TPU v7x, 32 devices: a whole 2x2x4 slice. The times are simulated.
32 devices in a mesh: section: 2 (over y), seq: 16 (over z, x, core).
Axes of the slice: x: 2, y: 2, z: 4, core: 2. Of those that a mesh axis runs over, the one named last changes fastest.
Arguments:
- queries: bfloat16 [2, 2048, 1024], P('section', 'seq'), may hold values from -35 to 35
- keys: bfloat16 [2, 2048, 1024], P('section', 'seq'), may hold values from -4 to 4
- values: bfloat16 [2, 2048, 1024], P('section', 'seq'), may hold values from -6 to 6
- upstream: bfloat16 [2, 2048, 1024], P('section', 'seq'), may hold values from -6 to 6
- neighbours: int32 [16, 6], replicated, may hold values from 0 to 15, as said below
- counts: int32 [16], replicated, may hold values from 1 to 6, as said below
Outputs:
- query_grad: bfloat16 [2, 2048, 1024], P('section', 'seq')
- key_grad: bfloat16 [2, 2048, 1024], P('section', 'seq')
- value_grad: bfloat16 [2, 2048, 1024], P('section', 'seq')
Inputs may be any that keep to these rules, and one draw needn't show every extreme that they name: Row a lists 6 different tiles, the first being a itself; only the first counts[a] of them are neighbours of a. `counts`: some tile has 6 neighbour tiles and some tile has only itself.
All inputs are finite; a program needn't handle non-finite values.
Results may differ from a plain program's by a relative error of at most 0.009.
Values may be sent and summed in bfloat16 or wider, within the bound.
A program may use at most 64 MiB of HBM per device.

v0:
```python
import jax
import jax.numpy as jnp
from jax import lax
from jax.sharding import PartitionSpec as P

HEADS = 16
DH = 64
TILE = 128
MAXNB = 6
MASKED = -1e30


def from_behind(block, axis, distance):
    devices = range(lax.axis_size(axis))
    route = [((i - distance) % len(devices), i) for i in devices]
    return lax.ppermute(block, axis, route)


def per_device(queries, keys, values, upstream, neighbours, counts):
    seq_count = lax.axis_size("seq")
    group_count = seq_count // HEADS
    row_count = queries.shape[1]
    model_width = queries.shape[2]
    quarter_rows = row_count // group_count
    unit_rows = min(quarter_rows, TILE)
    tile_count = neighbours.shape[0]
    my_group = lax.axis_index("seq") // HEADS
    adjoint = from_behind(upstream, "section", -1)

    def to_slots(block):
        return (
            block[0]
            .reshape(group_count, quarter_rows, HEADS, DH)
            .transpose(0, 2, 3, 1)
            .reshape(group_count * HEADS, DH, quarter_rows)
        )

    query_recv, adjoint_recv = (
        lax.all_to_all(to_slots(queries), "seq", split_axis=0, concat_axis=2, tiled=True),
        lax.all_to_all(to_slots(adjoint), "seq", split_axis=0, concat_axis=2, tiled=True),
    )
    query_cols = query_recv[0]
    adjoint_cols = adjoint_recv[0]

    def spread_rows(block):
        heads_first = block[0].reshape(row_count, HEADS, DH).transpose(1, 2, 0)
        return jnp.broadcast_to(heads_first[None], (group_count, HEADS, DH, row_count)).reshape(
            group_count * HEADS, DH, row_count
        )

    key_recv, value_recv = (
        lax.all_to_all(spread_rows(keys), "seq", split_axis=0, concat_axis=2, tiled=True),
        lax.all_to_all(spread_rows(values), "seq", split_axis=0, concat_axis=2, tiled=True),
    )
    key_cols = key_recv[0]
    value_cols = value_recv[0]
    key_tiles = key_cols.reshape(DH, tile_count, TILE).transpose(1, 0, 2)
    value_tiles = value_cols.reshape(DH, tile_count, TILE).transpose(1, 0, 2)
    query_total = seq_count * quarter_rows
    unit_count = query_total // unit_rows
    per_batch = min(unit_count, max(1, 512 // unit_rows))
    batch_count = unit_count // per_batch
    first_row = jnp.arange(unit_count, dtype=jnp.int32) * unit_rows
    source = first_row // quarter_rows
    offset = first_row % quarter_rows
    global_row = source * row_count + my_group * quarter_rows + offset
    unit_tiles = (global_row // TILE).reshape(batch_count, per_batch)

    def by_unit(cols):
        return cols.reshape(DH, batch_count, per_batch, unit_rows).transpose(1, 2, 0, 3)

    valid_table = (jnp.arange(MAXNB, dtype=jnp.int32)[None, :] < counts[:, None]).astype(
        jnp.float32
    )
    score_scale = DH ** (-0.5)
    tile_numbers = jnp.arange(tile_count, dtype=jnp.int32)

    def tile_sweep(carried, inputs):
        key_acc, value_acc = carried
        query_blk, adjoint_blk, tile_ids = inputs
        chosen = neighbours[tile_ids]
        alive_slots = valid_table[tile_ids][:, :, None, None]
        key_blk = key_tiles[chosen]
        value_blk = value_tiles[chosen]
        scores = (
            jnp.einsum("bei,bsej->bsij", query_blk, key_blk, preferred_element_type=jnp.float32)
            * score_scale
        )
        scores = jnp.where(alive_slots > 0, scores, MASKED)
        row_peak = jnp.max(scores, axis=(1, 3), keepdims=True)
        weights = jnp.exp(scores - row_peak) * alive_slots
        prob_full = weights / jnp.sum(weights, axis=(1, 3), keepdims=True)
        probs_low = prob_full.astype(jnp.bfloat16)
        dprobs = jnp.einsum(
            "bei,bsej->bsij", adjoint_blk, value_blk, preferred_element_type=jnp.float32
        )
        delta_sum = jnp.sum(prob_full * dprobs, axis=(1, 3), keepdims=True)
        dscores = (prob_full * (dprobs - delta_sum) * score_scale).astype(jnp.bfloat16)
        query_out = jnp.einsum(
            "bsij,bsej->bei", dscores, key_blk, preferred_element_type=jnp.float32
        ).astype(jnp.bfloat16)
        key_terms = jnp.einsum(
            "bsij,bei->bsej", dscores, query_blk, preferred_element_type=jnp.float32
        )
        value_terms = jnp.einsum(
            "bsij,bei->bsej", probs_low, adjoint_blk, preferred_element_type=jnp.float32
        )
        flat_ids = chosen.reshape(-1)
        picker = (flat_ids[None, :] == tile_numbers[:, None]).astype(jnp.float32)
        key_acc = key_acc + jnp.einsum(
            "tn,nej->tej",
            picker,
            key_terms.reshape(-1, DH, TILE),
            precision=lax.Precision.HIGHEST,
            preferred_element_type=jnp.float32,
        )
        value_acc = value_acc + jnp.einsum(
            "tn,nej->tej",
            picker,
            value_terms.reshape(-1, DH, TILE),
            precision=lax.Precision.HIGHEST,
            preferred_element_type=jnp.float32,
        )
        return ((key_acc, value_acc), query_out)

    empty_grad = jnp.zeros((tile_count, DH, TILE), jnp.float32)
    (key_acc, value_acc), query_units = lax.scan(
        tile_sweep,
        (empty_grad, empty_grad),
        (by_unit(query_cols), by_unit(adjoint_cols), unit_tiles),
    )
    query_send = (
        query_units.reshape(seq_count, quarter_rows // unit_rows, DH, unit_rows)
        .transpose(0, 2, 1, 3)
        .reshape(seq_count, 1, DH, quarter_rows)
    )
    query_back = lax.all_to_all(query_send, "seq", split_axis=0, concat_axis=1, tiled=True)
    query_grad = (
        query_back[0]
        .reshape(group_count, HEADS, DH, quarter_rows)
        .transpose(0, 3, 1, 2)
        .reshape(1, row_count, model_width)
    )

    def by_source(grad):
        return (
            grad.reshape(seq_count, row_count // TILE, DH, TILE)
            .transpose(0, 2, 1, 3)
            .reshape(seq_count, 1, DH, row_count)
        )

    got_key, got_value = (
        lax.all_to_all(
            by_source(key_acc).astype(jnp.bfloat16), "seq", split_axis=0, concat_axis=1, tiled=True
        ).astype(jnp.float32),
        lax.all_to_all(
            by_source(value_acc).astype(jnp.bfloat16),
            "seq",
            split_axis=0,
            concat_axis=1,
            tiled=True,
        ).astype(jnp.float32),
    )

    def finish_rows(got):
        summed = jnp.sum(got[0].reshape(group_count, HEADS, DH, row_count), axis=0)
        return summed.transpose(2, 0, 1).reshape(1, row_count, model_width).astype(jnp.bfloat16)

    key_grad = finish_rows(got_key)
    value_grad = finish_rows(got_value)
    return (query_grad, key_grad, value_grad)


def solution(mesh):
    in_specs = (
        P("section", "seq", None),
        P("section", "seq", None),
        P("section", "seq", None),
        P("section", "seq", None),
        P(),
        P(),
    )
    out_specs = (P("section", "seq", None), P("section", "seq", None), P("section", "seq", None))
    return jax.shard_map(
        per_device, mesh=mesh, in_specs=in_specs, out_specs=out_specs, check_vma=False
    )
```

profile of v0, /device:TPU:0, one launch (start us, length us, event | category | flops | bytes accessed | tf_op | source)
XLA Modules:
  0.0 162.7 jit_solution(16621503994922736800)
XLA Ops:
  0.7 1.8 %copy.46 = bf16[1,128,1024]{1,2,0:T(8,128)(2,1)} copy(bf16[1,128,1024]{2,1,0:T(8,128)(2,1)} %param.9) | data formatting | bytes 524288 | tf_op args[1]
  2.5 7.4 %all-to-all-start.1 = ((bf16[16,64,128]{2,1,0:T(8,128)(2,1)}), bf16[16,64,128]{2,1,0:T(8,128)(2,1)S(1)}, u32[]{:S(2)}, u32[]{:S(2)}) async-start(bf16[16,64,128]{2,1,0:T(8,128)(2,1)} %bitcast.8), calls=%async_computation.1 | async-start | bytes 524288 | tf_op jit(solution)/shard_map/all_to_all | solution.py:52
  9.9 1.8 %copy.47 = bf16[1,128,1024]{1,2,0:T(8,128)(2,1)} copy(bf16[1,128,1024]{2,1,0:T(8,128)(2,1)} %param.10) | data formatting | bytes 524288 | tf_op args[2]
  11.7 8.2 %all-to-all-done.1 = bf16[16,64,128]{2,1,0:T(8,128)(2,1)S(1)} async-done(((bf16[16,64,128]{2,1,0:T(8,128)(2,1)}), bf16[16,64,128]{2,1,0:T(8,128)(2,1)S(1)}, u32[]{:S(2)}, u32[]{:S(2)}) %all-to-all-start.1) | async-done | bytes 262176 | tf_op jit(solution)/shard_map/all_to_all | solution.py:52
  19.9 3.5 %all-to-all-start.2 = ((bf16[16,64,128]{2,1,0:T(8,128)(2,1)}), bf16[16,64,128]{2,1,0:T(8,128)(2,1)S(1)}, u32[]{:S(2)}, u32[]{:S(2)}) async-start(bf16[16,64,128]{2,1,0:T(8,128)(2,1)} %bitcast.10), calls=%async_computation.2 | async-start | bytes 524288 | tf_op jit(solution)/shard_map/all_to_all | solution.py:53
  23.5 0.8 copy.45
  24.3 9.1 %all-to-all-done.2 = bf16[16,64,128]{2,1,0:T(8,128)(2,1)S(1)} async-done(((bf16[16,64,128]{2,1,0:T(8,128)(2,1)}), bf16[16,64,128]{2,1,0:T(8,128)(2,1)S(1)}, u32[]{:S(2)}, u32[]{:S(2)}) %all-to-all-start.2) | async-done | bytes 262176 | tf_op jit(solution)/shard_map/all_to_all | solution.py:53
  33.4 3.5 %all-to-all-start = ((bf16[16,64,128]{2,1,0:T(8,128)(2,1)}), bf16[16,64,128]{2,1,0:T(8,128)(2,1)S(1)}, u32[]{:S(2)}, u32[]{:S(2)}) async-start(bf16[16,64,128]{2,1,0:T(8,128)(2,1)} %bitcast.2), calls=%async_computation | async-start | bytes 524288 | tf_op jit(solution)/shard_map/all_to_all | solution.py:39
  37.2 1.6 collective-permute-start
  38.7 7.1 %collective-permute-done = bf16[1,128,1024]{1,2,0:T(8,128)(2,1)} collective-permute-done((bf16[1,128,1024]{1,2,0:T(8,128)(2,1)S(1)}, bf16[1,128,1024]{1,2,0:T(8,128)(2,1)}, u32[]{:S(2)}, u32[]{:S(2)}) %collective-permute-start) | collective-permute-done | bytes 262176 | tf_op jit(solution)/shard_map/ppermute | solution.py:16
  45.8 1.1 all-to-all-done
  46.9 4.7 %all-to-all-start.3 = ((bf16[16,64,128]{2,1,0:T(8,128)(2,1)}), bf16[16,64,128]{2,1,0:T(8,128)(2,1)}, u32[]{:S(2)}, u32[]{:S(2)}) async-start(bf16[16,64,128]{2,1,0:T(8,128)(2,1)} %bitcast.13), calls=%async_computation.3 | async-start | bytes 524288 | tf_op jit(solution)/shard_map/all_to_all | solution.py:40
  52.4 9.3 %all-to-all-done.3 = bf16[16,64,128]{2,1,0:T(8,128)(2,1)} async-done(((bf16[16,64,128]{2,1,0:T(8,128)(2,1)}), bf16[16,64,128]{2,1,0:T(8,128)(2,1)}, u32[]{:S(2)}, u32[]{:S(2)}) %all-to-all-start.3) | async-done | bytes 262176 | tf_op jit(solution)/shard_map/all_to_all | solution.py:40
  61.8 58.4 %while.15 = (s32[]{:T(128)}, f32[16,64,128]{2,0,1:T(8,128)}, f32[16,64,128]{2,0,1:T(8,128)}, bf16[4,4,64,128]{3,2,1,0:T(8,128)(2,1)}, s32[4,4]{1,0:T(4,128)}, /*...) while((s32[]{:T(128)}, f32[16,64,128]{2,0,1:T(8,128)}, ...), condition=%wide.region_4.5_spmd.clone, body=%wide.region_0.4_spmd.clone.sunk | while | flops 336365120 | bytes 25971868 | solution.py:127
  63.8 0.7 fusion.89
  66.0 1.3 fusion.94
  67.9 2.3 %convolution_add_fusion.5 = f32[16,64,128]{2,0,1:T(8,128)} fusion(f32[24,64,128]{2,1,0:T(8,128)S(1)} %bitcast.200, f32[16,64,128]{2,0,1:T(8,128)} %get-tuple-element.266, pred[]{:T(512)S(6)} %compare.14, s32[24]{0:T(128)} %eq.43), kind=kOutput, calls=%fused_computation.19.clone.1 | convolution fusion | flops 38011264 | bytes 1835105 | tf_op jit(solution)/shard_map/while/body/eval_jaxpr/tn,nej->tej/dot_general | solution.py:117
  70.2 0.7 gather_fusion.3
  71.0 1.5 fusion.91
  74.2 1.0 convolution_add_fusion.4
  75.1 0.9 fusion.95
  80.2 1.3 fusion.94
  82.2 2.7 %convolution_add_fusion.5 = f32[16,64,128]{2,0,1:T(8,128)} fusion(f32[24,64,128]{2,1,0:T(8,128)S(1)} %bitcast.200, f32[16,64,128]{2,0,1:T(8,128)} %get-tuple-element.266, pred[]{:T(512)S(6)} %compare.14, s32[24]{0:T(128)} %eq.43), kind=kOutput, calls=%fused_computation.19.clone.1 | convolution fusion | flops 38011264 | bytes 1835105 | tf_op jit(solution)/shard_map/while/body/eval_jaxpr/tn,nej->tej/dot_general | solution.py:117
  84.9 0.7 gather_fusion.3
  85.7 1.5 fusion.91
  88.9 1.0 convolution_add_fusion.4
  89.8 0.9 fusion.95
  95.0 1.3 fusion.94
  96.9 2.7 %convolution_add_fusion.5 = f32[16,64,128]{2,0,1:T(8,128)} fusion(f32[24,64,128]{2,1,0:T(8,128)S(1)} %bitcast.200, f32[16,64,128]{2,0,1:T(8,128)} %get-tuple-element.266, pred[]{:T(512)S(6)} %compare.14, s32[24]{0:T(128)} %eq.43), kind=kOutput, calls=%fused_computation.19.clone.1 | convolution fusion | flops 38011264 | bytes 1835105 | tf_op jit(solution)/shard_map/while/body/eval_jaxpr/tn,nej->tej/dot_general | solution.py:117
  99.7 0.7 gather_fusion.3
  100.4 1.5 fusion.91
  103.6 1.0 convolution_add_fusion.4
  104.6 0.9 fusion.95
  109.7 1.3 fusion.94
  111.7 2.7 %convolution_add_fusion.5 = f32[16,64,128]{2,0,1:T(8,128)} fusion(f32[24,64,128]{2,1,0:T(8,128)S(1)} %bitcast.200, f32[16,64,128]{2,0,1:T(8,128)} %get-tuple-element.266, pred[]{:T(512)S(6)} %compare.14, s32[24]{0:T(128)} %eq.43), kind=kOutput, calls=%fused_computation.19.clone.1 | convolution fusion | flops 38011264 | bytes 1835105 | tf_op jit(solution)/shard_map/while/body/eval_jaxpr/tn,nej->tej/dot_general | solution.py:117
  114.4 0.7 gather_fusion.3
  115.1 1.5 fusion.91
  118.3 1.0 convolution_add_fusion.4
  119.3 0.9 fusion.95
  120.2 2.0 %copy.71 = bf16[16,64,128]{2,1,0:T(8,128)(2,1)} copy(f32[16,64,128]{2,0,1:T(8,128)} %get-tuple-element.68) | data formatting | bytes 786432 | tf_op jit(solution)/shard_map/while | solution.py:127
  122.2 3.5 %all-to-all-start.5 = ((bf16[16,1,64,128]{3,2,1,0:T(8,128)(2,1)}), bf16[16,1,64,128]{3,2,1,0:T(8,128)(2,1)S(1)}, u32[]{:S(2)}, u32[]{:S(2)}) async-start(bf16[16,1,64,128]{3,2,1,0:T(8,128)(2,1)} %bitcast.141), calls=%async_computation.5 | async-start | bytes 524288 | tf_op jit(solution)/shard_map/all_to_all | solution.py:153
  125.9 9.8 %all-to-all-done.5 = bf16[16,1,64,128]{3,2,1,0:T(8,128)(2,1)S(1)} async-done(((bf16[16,1,64,128]{3,2,1,0:T(8,128)(2,1)}), bf16[16,1,64,128]{3,2,1,0:T(8,128)(2,1)S(1)}, u32[]{:S(2)}, u32[]{:S(2)}) %all-to-all-start.5) | async-done | bytes 262176 | tf_op jit(solution)/shard_map/all_to_all | solution.py:153
  135.7 12.7 %all_to_all.78 = bf16[16,1,64,128]{3,2,1,0:T(8,128)(2,1)S(1)} all-to-all(bf16[16,1,64,128]{3,2,1,0:T(8,128)(2,1)S(1)} %bitcast.203), channel_id=1, replica_groups=mesh['section'=2,'seq'=16] {'seq'}, dimensions={0} | all-to-all | bytes 524288 | tf_op jit(solution)/shard_map/all_to_all | solution.py:156
  148.4 3.5 %all-to-all-start.4 = ((bf16[16,1,64,128]{3,2,1,0:T(8,128)(2,1)}), bf16[16,1,64,128]{3,2,1,0:T(8,128)(2,1)S(1)}, u32[]{:S(2)}, u32[]{:S(2)}) async-start(bf16[16,1,64,128]{3,2,1,0:T(8,128)(2,1)} %bitcast.18), calls=%async_computation.4 | async-start | bytes 524288 | tf_op jit(solution)/shard_map/all_to_all | solution.py:137
  151.9 0.9 copy.53
  152.8 0.8 copy.54
  153.6 8.3 %all-to-all-done.4 = bf16[16,1,64,128]{3,2,1,0:T(8,128)(2,1)S(1)} async-done(((bf16[16,1,64,128]{3,2,1,0:T(8,128)(2,1)}), bf16[16,1,64,128]{3,2,1,0:T(8,128)(2,1)S(1)}, u32[]{:S(2)}, u32[]{:S(2)}) %all-to-all-start.4) | async-done | bytes 262176 | tf_op jit(solution)/shard_map/all_to_all | solution.py:137
  161.9 0.8 copy.52
  (138 shorter events, 25.9 us)
Async XLA Ops:
  0.6 22.8 %copy-start.6 = (bf16[1,128,1024]{2,1,0:T(8,128)(2,1)S(1)}, bf16[1,128,1024]{2,1,0:T(8,128)(2,1)}, u32[]{:S(2)}) copy-start(bf16[1,128,1024]{2,1,0:T(8,128)(2,1)} %param.8) | copy-start | bytes 786436
  0.6 36.3 %copy-start.7 = (bf16[1,128,1024]{2,1,0:T(8,128)(2,1)S(1)}, bf16[1,128,1024]{2,1,0:T(8,128)(2,1)}, u32[]{:S(2)}) copy-start(bf16[1,128,1024]{2,1,0:T(8,128)(2,1)} %param.11) | copy-start | bytes 786436
  2.5 17.4 %all-to-all-start.1 = ((bf16[16,64,128]{2,1,0:T(8,128)(2,1)}), bf16[16,64,128]{2,1,0:T(8,128)(2,1)S(1)}, u32[]{:S(2)}, u32[]{:S(2)}) async-start(bf16[16,64,128]{2,1,0:T(8,128)(2,1)} %bitcast.8), calls=%async_computation.1 | async-start | bytes 524288 | tf_op jit(solution)/shard_map/all_to_all | solution.py:52
  9.9 41.8 %copy-start.11 = (s32[16,6]{0,1:T(8,128)S(1)}, s32[16,6]{0,1:T(8,128)}, u32[]{:S(2)}) copy-start(s32[16,6]{0,1:T(8,128)} %param.12) | copy-start | bytes 1156
  19.9 13.5 %all-to-all-start.2 = ((bf16[16,64,128]{2,1,0:T(8,128)(2,1)}), bf16[16,64,128]{2,1,0:T(8,128)(2,1)S(1)}, u32[]{:S(2)}, u32[]{:S(2)}) async-start(bf16[16,64,128]{2,1,0:T(8,128)(2,1)} %bitcast.10), calls=%async_computation.2 | async-start | bytes 524288 | tf_op jit(solution)/shard_map/all_to_all | solution.py:53
  33.4 13.5 %all-to-all-start = ((bf16[16,64,128]{2,1,0:T(8,128)(2,1)}), bf16[16,64,128]{2,1,0:T(8,128)(2,1)S(1)}, u32[]{:S(2)}, u32[]{:S(2)}) async-start(bf16[16,64,128]{2,1,0:T(8,128)(2,1)} %bitcast.2), calls=%async_computation | async-start | bytes 524288 | tf_op jit(solution)/shard_map/all_to_all | solution.py:39
  37.2 8.7 %collective-permute-start = (bf16[1,128,1024]{1,2,0:T(8,128)(2,1)S(1)}, bf16[1,128,1024]{1,2,0:T(8,128)(2,1)}, u32[]{:S(2)}, u32[]{:S(2)}) collective-permute-start(bf16[1,128,1024]{1,2,0:T(8,128)(2,1)S(1)} %copy.48), channel_id=1, source_target_pairs={{16,0},{0,16},{17,1},{1,17},{18,2},{2,18},{19,3},{3,19},{20,4},{4,... | collective-permute-start | bytes 786440 | tf_op jit(solution)/shard_map/ppermute | solution.py:16
  46.9 14.8 %all-to-all-start.3 = ((bf16[16,64,128]{2,1,0:T(8,128)(2,1)}), bf16[16,64,128]{2,1,0:T(8,128)(2,1)}, u32[]{:S(2)}, u32[]{:S(2)}) async-start(bf16[16,64,128]{2,1,0:T(8,128)(2,1)} %bitcast.13), calls=%async_computation.3 | async-start | bytes 524288 | tf_op jit(solution)/shard_map/all_to_all | solution.py:40
  63.1 0.6 copy-start.5
  65.6 1.7 %copy-start.3 = (f32[4,128]{1,0:T(4,128)}, f32[4,128]{1,0:T(4,128)S(1)}, u32[]{:S(2)}) copy-start(f32[4,128]{1,0:T(4,128)S(1)} %get-tuple-element.248) | copy-start | bytes 6148 | tf_op jit(solution)/shard_map/while
  66.0 1.4 copy-start.8
  67.9 3.0 %copy-start.4 = (f32[4,128]{1,0:T(4,128)S(1)}, f32[4,128]{1,0:T(4,128)}, u32[]{:S(2)}) copy-start(f32[4,128]{1,0:T(4,128)} %copy-done.3) | copy-start | bytes 6148 | tf_op jit(solution)/shard_map/while
  71.0 1.5 copy-start.9
  73.1 1.0 copy-start
  73.1 1.0 copy-start.10
  75.1 0.9 copy-start.1
  77.4 0.6 copy-start.5
  79.9 1.7 %copy-start.3 = (f32[4,128]{1,0:T(4,128)}, f32[4,128]{1,0:T(4,128)S(1)}, u32[]{:S(2)}) copy-start(f32[4,128]{1,0:T(4,128)S(1)} %get-tuple-element.248) | copy-start | bytes 6148 | tf_op jit(solution)/shard_map/while
  80.2 1.4 copy-start.8
  82.2 3.5 %copy-start.4 = (f32[4,128]{1,0:T(4,128)S(1)}, f32[4,128]{1,0:T(4,128)}, u32[]{:S(2)}) copy-start(f32[4,128]{1,0:T(4,128)} %copy-done.3) | copy-start | bytes 6148 | tf_op jit(solution)/shard_map/while
  85.7 1.5 copy-start.9
  87.8 1.0 copy-start
  87.8 1.0 copy-start.10
  89.8 0.9 copy-start.1
  92.1 0.6 copy-start.5
  94.6 1.7 %copy-start.3 = (f32[4,128]{1,0:T(4,128)}, f32[4,128]{1,0:T(4,128)S(1)}, u32[]{:S(2)}) copy-start(f32[4,128]{1,0:T(4,128)S(1)} %get-tuple-element.248) | copy-start | bytes 6148 | tf_op jit(solution)/shard_map/while
  95.0 1.4 copy-start.8
  96.9 3.5 %copy-start.4 = (f32[4,128]{1,0:T(4,128)S(1)}, f32[4,128]{1,0:T(4,128)}, u32[]{:S(2)}) copy-start(f32[4,128]{1,0:T(4,128)} %copy-done.3) | copy-start | bytes 6148 | tf_op jit(solution)/shard_map/while
  100.4 1.5 copy-start.9
  102.5 1.0 copy-start
  102.6 1.0 copy-start.10
  104.5 0.9 copy-start.1
  106.8 0.6 copy-start.5
  109.3 1.7 %copy-start.3 = (f32[4,128]{1,0:T(4,128)}, f32[4,128]{1,0:T(4,128)S(1)}, u32[]{:S(2)}) copy-start(f32[4,128]{1,0:T(4,128)S(1)} %get-tuple-element.248) | copy-start | bytes 6148 | tf_op jit(solution)/shard_map/while
  109.7 1.4 copy-start.8
  111.7 3.5 %copy-start.4 = (f32[4,128]{1,0:T(4,128)S(1)}, f32[4,128]{1,0:T(4,128)}, u32[]{:S(2)}) copy-start(f32[4,128]{1,0:T(4,128)} %copy-done.3) | copy-start | bytes 6148 | tf_op jit(solution)/shard_map/while
  115.1 1.5 copy-start.9
  117.3 1.0 copy-start
  117.3 1.0 copy-start.10
  119.3 0.9 copy-start.1
  120.2 5.5 %copy-start.2 = (f32[16,64,128]{2,0,1:T(8,128)S(1)}, f32[16,64,128]{2,0,1:T(8,128)}, u32[]{:S(2)}) copy-start(f32[16,64,128]{2,0,1:T(8,128)} %get-tuple-element.69) | copy-start | bytes 1572868
  122.2 13.5 %all-to-all-start.5 = ((bf16[16,1,64,128]{3,2,1,0:T(8,128)(2,1)}), bf16[16,1,64,128]{3,2,1,0:T(8,128)(2,1)S(1)}, u32[]{:S(2)}, u32[]{:S(2)}) async-start(bf16[16,1,64,128]{3,2,1,0:T(8,128)(2,1)} %bitcast.141), calls=%async_computation.5 | async-start | bytes 524288 | tf_op jit(solution)/shard_map/all_to_all | solution.py:153
  148.4 13.5 %all-to-all-start.4 = ((bf16[16,1,64,128]{3,2,1,0:T(8,128)(2,1)}), bf16[16,1,64,128]{3,2,1,0:T(8,128)(2,1)S(1)}, u32[]{:S(2)}, u32[]{:S(2)}) async-start(bf16[16,1,64,128]{3,2,1,0:T(8,128)(2,1)} %bitcast.18), calls=%async_computation.4 | async-start | bytes 524288 | tf_op jit(solution)/shard_map/all_to_all | solution.py:137
where the time goes:
time: 164 us; the launch traced here: 163 us
  waiting for transfers between devices  52.9 us (32%)
  matrix products  33 us (20%)
  starting transfers between devices  27.8 us (17%)
  local copies, waits for them, and re-layouts  24.8 us (15%)
  blocking collectives  12.7 us (8%)
  other arithmetic  10.2 us (6%)
    all_to_all x1, blocking collectives, per_device(): lax.all_to_all(by_source(value_acc).astype(jnp.bfloat16), 'seq', split_ax...  12.7 us
    dot_general x4, matrix products, tile_sweep(): jnp.einsum('tn,nej->tej', picker, value_terms.reshape(-1, DH, TILE), prec...  10.4 us
    all_to_all x1, waiting for transfers between devices, per_device(): lax.all_to_all(by_source(key_acc).astype(jnp.bfloat16), 'seq', split_axis...  9.79 us
    all_to_all x1, waiting for transfers between devices, per_device(): lax.all_to_all(to_slots(adjoint), 'seq', split_axis=0, concat_axis=2, til...  9.33 us
    all_to_all x1, waiting for transfers between devices, per_device(): lax.all_to_all(spread_rows(values), 'seq', split_axis=0, concat_axis=2, t...  9.13 us
    all_to_all x1, waiting for transfers between devices, per_device(): lax.all_to_all(query_send, 'seq', split_axis=0, concat_axis=1, tiled=True)  8.28 us
    all_to_all x1, waiting for transfers between devices, per_device(): lax.all_to_all(spread_rows(keys), 'seq', split_axis=0, concat_axis=2, til...  8.21 us
    all_to_all x1, starting transfers between devices, per_device(): lax.all_to_all(spread_rows(keys), 'seq', split_axis=0, concat_axis=2, til...  7.39 us
  transfers between devices with their start and end apart: 7, of which 7 were waited for; matrix products, arithmetic and copies ran while one was open for 3% of the time, Pallas kernels for 0%

commit v1 on v0

--- a/solution.py
+++ b/solution.py
@@ -134,7 +134,10 @@
         .transpose(0, 2, 1, 3)
         .reshape(seq_count, 1, DH, quarter_rows)
     )
-    query_back = lax.all_to_all(query_send, "seq", split_axis=0, concat_axis=1, tiled=True)
+    count = lax.axis_size("seq")
+    blocks = jnp.stack(jnp.split(query_send, count, axis=0), axis=0)
+    blocks = lax.all_to_all(blocks, "seq", split_axis=0, concat_axis=0)
+    query_back = jnp.concatenate(blocks, axis=1)
     query_grad = (
         query_back[0]
         .reshape(group_count, HEADS, DH, quarter_rows)

time: 164 us -> 186 us (1.13); the launches traced: 163 us -> 183 us
  local copies, waits for them, and re-layouts: 24.8 us -> 46.7 us
  blocking collectives: 12.7 us -> 0 us
  waiting for transfers between devices: 52.9 us -> 60.3 us
  starting transfers between devices: 27.8 us -> 31.4 us
    unnamed x16 -> x31, local copies, waits for them, and re-layouts: 7.3 us -> 27.2 us
    all_to_all x1 -> x0, blocking collectives: 12.7 us -> none  [per_device(): lax.all_to_all(by_source(value_acc).astype(jnp.bfloat16), 'seq', split_ax...]
    all_to_all x1 -> x2, waiting for transfers between devices: 8.28 us -> 16.3 us  [the longest x1 8.28 us: per_device(): lax.all_to_all(by_source(value_acc).astype(jnp.bfloat16), 'seq', split_ax...]
    all_to_all x1 -> x2, starting transfers between devices: 3.53 us -> 7.06 us  [the longest x1 3.53 us: per_device(): blocks = lax.all_to_all(blocks, 'seq', split_axis=0, concat_axis=0)]
  transfers between devices with their start and end apart: 7 -> 8, of which waited for: 7 -> 8; matrix products, arithmetic and copies ran while one was open for 3% -> 4% of each run, Pallas kernels for 0% -> 0%
where the time goes in v1:
time: 186 us; the launch traced here: 183 us
  waiting for transfers between devices  60.3 us (32%)
  local copies, waits for them, and re-layouts  46.7 us (25%)
  matrix products  33 us (18%)
  starting transfers between devices  31.4 us (17%)
  other arithmetic  10.2 us (5%)
    unnamed x31, local copies, waits for them, and re-layouts  27.2 us
    dot_general x4, matrix products, tile_sweep(): jnp.einsum('tn,nej->tej', picker, value_terms.reshape(-1, DH, TILE), prec...  10.4 us
    all_to_all x1, waiting for transfers between devices, per_device(): lax.all_to_all(to_slots(adjoint), 'seq', split_axis=0, concat_axis=2, til...  9.33 us
    all_to_all x1, waiting for transfers between devices, per_device(): lax.all_to_all(spread_rows(values), 'seq', split_axis=0, concat_axis=2, t...  9.13 us
    all_to_all x1, waiting for transfers between devices, per_device(): lax.all_to_all(by_source(key_acc).astype(jnp.bfloat16), 'seq', split_axis...  9.1 us
    all_to_all x1, waiting for transfers between devices, per_device(): lax.all_to_all(by_source(value_acc).astype(jnp.bfloat16), 'seq', split_ax...  8.28 us
    all_to_all x1, waiting for transfers between devices, per_device(): lax.all_to_all(spread_rows(keys), 'seq', split_axis=0, concat_axis=2, til...  8.21 us
    all_to_all x1, waiting for transfers between devices, per_device(): blocks = lax.all_to_all(blocks, 'seq', split_axis=0, concat_axis=0)  8.06 us
  transfers between devices with their start and end apart: 8, of which 8 were waited for; matrix products, arithmetic and copies ran while one was open for 4% of the time, Pallas kernels for 0%

profile of v1, /device:TPU:0, one launch (start us, length us, event | category | flops | bytes accessed | tf_op | source)
XLA Modules:
  0.0 182.9 jit_solution(11195937883788385844)
XLA Ops:
  0.7 1.8 %copy.61 = bf16[1,128,1024]{1,2,0:T(8,128)(2,1)} copy(bf16[1,128,1024]{2,1,0:T(8,128)(2,1)} %param.9) | data formatting | bytes 524288 | tf_op args[1]
  2.5 7.4 %all-to-all-start.1 = ((bf16[16,64,128]{2,1,0:T(8,128)(2,1)}), bf16[16,64,128]{2,1,0:T(8,128)(2,1)S(1)}, u32[]{:S(2)}, u32[]{:S(2)}) async-start(bf16[16,64,128]{2,1,0:T(8,128)(2,1)} %bitcast.8), calls=%async_computation.1 | async-start | bytes 524288 | tf_op jit(solution)/shard_map/all_to_all | solution.py:52
  9.9 1.8 copy.62
  11.7 8.2 %all-to-all-done.1 = bf16[16,64,128]{2,1,0:T(8,128)(2,1)S(1)} async-done(((bf16[16,64,128]{2,1,0:T(8,128)(2,1)}), bf16[16,64,128]{2,1,0:T(8,128)(2,1)S(1)}, u32[]{:S(2)}, u32[]{:S(2)}) %all-to-all-start.1) | async-done | bytes 262176 | tf_op jit(solution)/shard_map/all_to_all | solution.py:52
  19.9 3.5 %all-to-all-start.2 = ((bf16[16,64,128]{2,1,0:T(8,128)(2,1)}), bf16[16,64,128]{2,1,0:T(8,128)(2,1)S(1)}, u32[]{:S(2)}, u32[]{:S(2)}) async-start(bf16[16,64,128]{2,1,0:T(8,128)(2,1)} %bitcast.10), calls=%async_computation.2 | async-start | bytes 524288 | tf_op jit(solution)/shard_map/all_to_all | solution.py:53
  24.3 9.1 %all-to-all-done.2 = bf16[16,64,128]{2,1,0:T(8,128)(2,1)S(1)} async-done(((bf16[16,64,128]{2,1,0:T(8,128)(2,1)}), bf16[16,64,128]{2,1,0:T(8,128)(2,1)S(1)}, u32[]{:S(2)}, u32[]{:S(2)}) %all-to-all-start.2) | async-done | bytes 262176 | tf_op jit(solution)/shard_map/all_to_all | solution.py:53
  33.4 3.5 %all-to-all-start = ((bf16[16,64,128]{2,1,0:T(8,128)(2,1)}), bf16[16,64,128]{2,1,0:T(8,128)(2,1)S(1)}, u32[]{:S(2)}, u32[]{:S(2)}) async-start(bf16[16,64,128]{2,1,0:T(8,128)(2,1)} %bitcast.2), calls=%async_computation | async-start | bytes 524288 | tf_op jit(solution)/shard_map/all_to_all | solution.py:39
  37.2 1.6 collective-permute-start
  38.7 7.1 %collective-permute-done = bf16[1,128,1024]{1,2,0:T(8,128)(2,1)} collective-permute-done((bf16[1,128,1024]{1,2,0:T(8,128)(2,1)S(1)}, bf16[1,128,1024]{1,2,0:T(8,128)(2,1)}, u32[]{:S(2)}, u32[]{:S(2)}) %collective-permute-start) | collective-permute-done | bytes 262176 | tf_op jit(solution)/shard_map/ppermute | solution.py:16
  45.8 1.1 all-to-all-done
  46.9 4.7 %all-to-all-start.3 = ((bf16[16,64,128]{2,1,0:T(8,128)(2,1)}), bf16[16,64,128]{2,1,0:T(8,128)(2,1)}, u32[]{:S(2)}, u32[]{:S(2)}) async-start(bf16[16,64,128]{2,1,0:T(8,128)(2,1)} %bitcast.13), calls=%async_computation.3 | async-start | bytes 524288 | tf_op jit(solution)/shard_map/all_to_all | solution.py:40
  52.4 9.3 %all-to-all-done.3 = bf16[16,64,128]{2,1,0:T(8,128)(2,1)} async-done(((bf16[16,64,128]{2,1,0:T(8,128)(2,1)}), bf16[16,64,128]{2,1,0:T(8,128)(2,1)}, u32[]{:S(2)}, u32[]{:S(2)}) %all-to-all-start.3) | async-done | bytes 262176 | tf_op jit(solution)/shard_map/all_to_all | solution.py:40
  61.8 58.5 %while.15 = (s32[]{:T(128)}, f32[16,64,128]{2,0,1:T(8,128)}, f32[16,64,128]{2,0,1:T(8,128)}, bf16[4,4,64,128]{3,2,1,0:T(8,128)(2,1)}, s32[4,4]{1,0:T(4,128)}, /*...) while((s32[]{:T(128)}, f32[16,64,128]{2,0,1:T(8,128)}, ...), condition=%wide.region_4.5_spmd.clone, body=%wide.region_0.4_spmd.clone.sunk | while | flops 336365120 | bytes 25971868 | solution.py:127
  66.0 1.3 fusion.94
  67.9 2.3 %convolution_add_fusion.5 = f32[16,64,128]{2,0,1:T(8,128)} fusion(f32[24,64,128]{2,1,0:T(8,128)S(1)} %bitcast.264, f32[16,64,128]{2,0,1:T(8,128)} %get-tuple-element.266, pred[]{:T(512)S(6)} %compare.14, s32[24]{0:T(128)} %eq.43), kind=kOutput, calls=%fused_computation.19.clone.1 | convolution fusion | flops 38011264 | bytes 1835105 | tf_op jit(solution)/shard_map/while/body/eval_jaxpr/tn,nej->tej/dot_general | solution.py:117
  71.0 1.5 fusion.91
  80.3 1.3 fusion.94
  82.2 2.7 %convolution_add_fusion.5 = f32[16,64,128]{2,0,1:T(8,128)} fusion(f32[24,64,128]{2,1,0:T(8,128)S(1)} %bitcast.264, f32[16,64,128]{2,0,1:T(8,128)} %get-tuple-element.266, pred[]{:T(512)S(6)} %compare.14, s32[24]{0:T(128)} %eq.43), kind=kOutput, calls=%fused_computation.19.clone.1 | convolution fusion | flops 38011264 | bytes 1835105 | tf_op jit(solution)/shard_map/while/body/eval_jaxpr/tn,nej->tej/dot_general | solution.py:117
  85.7 1.5 fusion.91
  95.0 1.3 fusion.94
  97.0 2.7 %convolution_add_fusion.5 = f32[16,64,128]{2,0,1:T(8,128)} fusion(f32[24,64,128]{2,1,0:T(8,128)S(1)} %bitcast.264, f32[16,64,128]{2,0,1:T(8,128)} %get-tuple-element.266, pred[]{:T(512)S(6)} %compare.14, s32[24]{0:T(128)} %eq.43), kind=kOutput, calls=%fused_computation.19.clone.1 | convolution fusion | flops 38011264 | bytes 1835105 | tf_op jit(solution)/shard_map/while/body/eval_jaxpr/tn,nej->tej/dot_general | solution.py:117
  100.5 1.5 fusion.91
  109.7 1.3 fusion.94
  111.7 2.7 %convolution_add_fusion.5 = f32[16,64,128]{2,0,1:T(8,128)} fusion(f32[24,64,128]{2,1,0:T(8,128)S(1)} %bitcast.264, f32[16,64,128]{2,0,1:T(8,128)} %get-tuple-element.266, pred[]{:T(512)S(6)} %compare.14, s32[24]{0:T(128)} %eq.43), kind=kOutput, calls=%fused_computation.19.clone.1 | convolution fusion | flops 38011264 | bytes 1835105 | tf_op jit(solution)/shard_map/while/body/eval_jaxpr/tn,nej->tej/dot_general | solution.py:117
  115.2 1.5 fusion.91
  120.2 1.4 constant_dynamic-update-slice_fusion.15
  121.6 1.3 constant_dynamic-update-slice_fusion.14
  123.0 1.3 constant_dynamic-update-slice_fusion.13
  124.3 1.3 constant_dynamic-update-slice_fusion.12
  125.6 1.3 constant_dynamic-update-slice_fusion.11
  126.9 1.3 constant_dynamic-update-slice_fusion.10
  128.2 1.3 constant_dynamic-update-slice_fusion.9
  129.6 1.3 constant_dynamic-update-slice_fusion.8
  130.9 1.3 constant_dynamic-update-slice_fusion.7
  132.2 1.3 constant_dynamic-update-slice_fusion.6
  133.5 1.3 constant_dynamic-update-slice_fusion.5
  134.9 1.3 constant_dynamic-update-slice_fusion.4
  136.2 1.3 constant_dynamic-update-slice_fusion.3
  137.5 1.3 constant_dynamic-update-slice_fusion.2
  138.8 1.3 constant_dynamic-update-slice_fusion.1
  140.2 1.3 constant_dynamic-update-slice_fusion
  141.5 3.5 %all-to-all-start.4 = ((bf16[16,1,1,64,128]{4,3,2,1,0:T(8,128)(2,1)}), bf16[16,1,1,64,128]{4,3,2,1,0:T(8,128)(2,1)S(1)}, u32[]{:S(2)}, u32[]{:S(2)}) async-start(bf16[16,1,1,64,128]{4,3,2,1,0:T(8,128)(2,1)} %constant_dynamic-update-slice_fusion), calls=%async_computation.4 | async-start | bytes 524288 | tf_op jit(solution)/shard_map/all_to_all | solution.py:139
  145.0 1.9 %copy.86 = bf16[16,64,128]{2,1,0:T(8,128)(2,1)} copy(f32[16,64,128]{2,0,1:T(8,128)} %get-tuple-element.68) | data formatting | bytes 786432 | tf_op jit(solution)/shard_map/while | solution.py:127
  146.9 8.1 %all-to-all-done.4 = bf16[16,1,1,64,128]{4,3,2,1,0:T(8,128)(2,1)S(1)} async-done(((bf16[16,1,1,64,128]{4,3,2,1,0:T(8,128)(2,1)}), bf16[16,1,1,64,128]{4,3,2,1,0:T(8,128)(2,1)S(1)}, u32[]{:S(2)}, u32[]{:S(2)}) %all-to-all-start.4) | async-done | bytes 262176 | tf_op jit(solution)/shard_map/all_to_all | solution.py:139
  155.0 3.5 %all-to-all-start.5 = ((bf16[16,1,64,128]{3,2,1,0:T(8,128)(2,1)}), bf16[16,1,64,128]{3,2,1,0:T(8,128)(2,1)S(1)}, u32[]{:S(2)}, u32[]{:S(2)}) async-start(bf16[16,1,64,128]{3,2,1,0:T(8,128)(2,1)} %bitcast.205), calls=%async_computation.5 | async-start | bytes 524288 | tf_op jit(solution)/shard_map/all_to_all | solution.py:156
  159.4 9.1 %all-to-all-done.5 = bf16[16,1,64,128]{3,2,1,0:T(8,128)(2,1)S(1)} async-done(((bf16[16,1,64,128]{3,2,1,0:T(8,128)(2,1)}), bf16[16,1,64,128]{3,2,1,0:T(8,128)(2,1)S(1)}, u32[]{:S(2)}, u32[]{:S(2)}) %all-to-all-start.5) | async-done | bytes 262176 | tf_op jit(solution)/shard_map/all_to_all | solution.py:156
  168.5 3.5 %all-to-all-start.6 = ((bf16[16,1,64,128]{3,2,1,0:T(8,128)(2,1)}), bf16[16,1,64,128]{3,2,1,0:T(8,128)(2,1)S(1)}, u32[]{:S(2)}, u32[]{:S(2)}) async-start(bf16[16,1,64,128]{3,2,1,0:T(8,128)(2,1)} %bitcast.206), calls=%async_computation.6 | async-start | bytes 524288 | tf_op jit(solution)/shard_map/all_to_all | solution.py:159
  173.8 8.3 %all-to-all-done.6 = bf16[16,1,64,128]{3,2,1,0:T(8,128)(2,1)S(1)} async-done(((bf16[16,1,64,128]{3,2,1,0:T(8,128)(2,1)}), bf16[16,1,64,128]{3,2,1,0:T(8,128)(2,1)S(1)}, u32[]{:S(2)}, u32[]{:S(2)}) %all-to-all-start.6) | async-done | bytes 262176 | tf_op jit(solution)/shard_map/all_to_all | solution.py:159
  (155 shorter events, 41.3 us)
Async XLA Ops:
  0.6 22.8 %copy-start.6 = (bf16[1,128,1024]{2,1,0:T(8,128)(2,1)S(1)}, bf16[1,128,1024]{2,1,0:T(8,128)(2,1)}, u32[]{:S(2)}) copy-start(bf16[1,128,1024]{2,1,0:T(8,128)(2,1)} %param.8) | copy-start | bytes 786436
  0.6 36.3 %copy-start.7 = (bf16[1,128,1024]{2,1,0:T(8,128)(2,1)S(1)}, bf16[1,128,1024]{2,1,0:T(8,128)(2,1)}, u32[]{:S(2)}) copy-start(bf16[1,128,1024]{2,1,0:T(8,128)(2,1)} %param.11) | copy-start | bytes 786436
  2.5 17.4 %all-to-all-start.1 = ((bf16[16,64,128]{2,1,0:T(8,128)(2,1)}), bf16[16,64,128]{2,1,0:T(8,128)(2,1)S(1)}, u32[]{:S(2)}, u32[]{:S(2)}) async-start(bf16[16,64,128]{2,1,0:T(8,128)(2,1)} %bitcast.8), calls=%async_computation.1 | async-start | bytes 524288 | tf_op jit(solution)/shard_map/all_to_all | solution.py:52
  9.9 41.8 %copy-start.11 = (s32[16,6]{0,1:T(8,128)S(1)}, s32[16,6]{0,1:T(8,128)}, u32[]{:S(2)}) copy-start(s32[16,6]{0,1:T(8,128)} %param.12) | copy-start | bytes 1156
  19.9 13.5 %all-to-all-start.2 = ((bf16[16,64,128]{2,1,0:T(8,128)(2,1)}), bf16[16,64,128]{2,1,0:T(8,128)(2,1)S(1)}, u32[]{:S(2)}, u32[]{:S(2)}) async-start(bf16[16,64,128]{2,1,0:T(8,128)(2,1)} %bitcast.10), calls=%async_computation.2 | async-start | bytes 524288 | tf_op jit(solution)/shard_map/all_to_all | solution.py:53
  33.4 13.5 %all-to-all-start = ((bf16[16,64,128]{2,1,0:T(8,128)(2,1)}), bf16[16,64,128]{2,1,0:T(8,128)(2,1)S(1)}, u32[]{:S(2)}, u32[]{:S(2)}) async-start(bf16[16,64,128]{2,1,0:T(8,128)(2,1)} %bitcast.2), calls=%async_computation | async-start | bytes 524288 | tf_op jit(solution)/shard_map/all_to_all | solution.py:39
  37.2 8.7 %collective-permute-start = (bf16[1,128,1024]{1,2,0:T(8,128)(2,1)S(1)}, bf16[1,128,1024]{1,2,0:T(8,128)(2,1)}, u32[]{:S(2)}, u32[]{:S(2)}) collective-permute-start(bf16[1,128,1024]{1,2,0:T(8,128)(2,1)S(1)} %copy.63), channel_id=1, source_target_pairs={{16,0},{0,16},{17,1},{1,17},{18,2},{2,18},{19,3},{3,19},{20,4},{4,... | collective-permute-start | bytes 786440 | tf_op jit(solution)/shard_map/ppermute | solution.py:16
  46.9 14.8 %all-to-all-start.3 = ((bf16[16,64,128]{2,1,0:T(8,128)(2,1)}), bf16[16,64,128]{2,1,0:T(8,128)(2,1)}, u32[]{:S(2)}, u32[]{:S(2)}) async-start(bf16[16,64,128]{2,1,0:T(8,128)(2,1)} %bitcast.13), calls=%async_computation.3 | async-start | bytes 524288 | tf_op jit(solution)/shard_map/all_to_all | solution.py:40
  63.1 0.6 copy-start.5
  65.6 1.7 copy-start.3
  66.0 1.4 copy-start.8
  67.9 3.0 %copy-start.4 = (f32[4,128]{1,0:T(4,128)S(1)}, f32[4,128]{1,0:T(4,128)}, u32[]{:S(2)}) copy-start(f32[4,128]{1,0:T(4,128)} %copy-done.3) | copy-start | bytes 6148 | tf_op jit(solution)/shard_map/while
  71.0 1.5 copy-start.9
  73.1 1.0 copy-start
  73.1 1.0 copy-start.10
  75.1 0.9 copy-start.1
  77.4 0.6 copy-start.5
  79.9 1.7 copy-start.3
  80.3 1.4 copy-start.8
  82.2 3.5 %copy-start.4 = (f32[4,128]{1,0:T(4,128)S(1)}, f32[4,128]{1,0:T(4,128)}, u32[]{:S(2)}) copy-start(f32[4,128]{1,0:T(4,128)} %copy-done.3) | copy-start | bytes 6148 | tf_op jit(solution)/shard_map/while
  85.7 1.5 copy-start.9
  87.8 1.0 copy-start
  87.9 1.0 copy-start.10
  89.9 0.9 copy-start.1
  92.1 0.6 copy-start.5
  94.6 1.7 copy-start.3
  95.0 1.4 copy-start.8
  97.0 3.5 %copy-start.4 = (f32[4,128]{1,0:T(4,128)S(1)}, f32[4,128]{1,0:T(4,128)}, u32[]{:S(2)}) copy-start(f32[4,128]{1,0:T(4,128)} %copy-done.3) | copy-start | bytes 6148 | tf_op jit(solution)/shard_map/while
  100.4 1.5 copy-start.9
  102.6 1.0 copy-start
  102.6 1.0 copy-start.10
  104.6 0.9 copy-start.1
  106.9 0.6 copy-start.5
  109.3 1.7 copy-start.3
  109.7 1.4 copy-start.8
  111.7 3.5 %copy-start.4 = (f32[4,128]{1,0:T(4,128)S(1)}, f32[4,128]{1,0:T(4,128)}, u32[]{:S(2)}) copy-start(f32[4,128]{1,0:T(4,128)} %copy-done.3) | copy-start | bytes 6148 | tf_op jit(solution)/shard_map/while
  115.2 1.5 copy-start.9
  117.3 1.0 copy-start
  117.3 1.0 copy-start.10
  119.3 0.9 copy-start.1
  120.2 38.3 %copy-start.2 = (f32[16,64,128]{2,0,1:T(8,128)S(1)}, f32[16,64,128]{2,0,1:T(8,128)}, u32[]{:S(2)}) copy-start(f32[16,64,128]{2,0,1:T(8,128)} %get-tuple-element.69) | copy-start | bytes 1572868
  141.5 13.5 %all-to-all-start.4 = ((bf16[16,1,1,64,128]{4,3,2,1,0:T(8,128)(2,1)}), bf16[16,1,1,64,128]{4,3,2,1,0:T(8,128)(2,1)S(1)}, u32[]{:S(2)}, u32[]{:S(2)}) async-start(bf16[16,1,1,64,128]{4,3,2,1,0:T(8,128)(2,1)} %constant_dynamic-update-slice_fusion), calls=%async_computation.4 | async-start | bytes 524288 | tf_op jit(solution)/shard_map/all_to_all | solution.py:139
  155.0 13.5 %all-to-all-start.5 = ((bf16[16,1,64,128]{3,2,1,0:T(8,128)(2,1)}), bf16[16,1,64,128]{3,2,1,0:T(8,128)(2,1)S(1)}, u32[]{:S(2)}, u32[]{:S(2)}) async-start(bf16[16,1,64,128]{3,2,1,0:T(8,128)(2,1)} %bitcast.205), calls=%async_computation.5 | async-start | bytes 524288 | tf_op jit(solution)/shard_map/all_to_all | solution.py:156
  168.5 13.5 %all-to-all-start.6 = ((bf16[16,1,64,128]{3,2,1,0:T(8,128)(2,1)}), bf16[16,1,64,128]{3,2,1,0:T(8,128)(2,1)S(1)}, u32[]{:S(2)}, u32[]{:S(2)}) async-start(bf16[16,1,64,128]{3,2,1,0:T(8,128)(2,1)} %bitcast.206), calls=%async_computation.6 | async-start | bytes 524288 | tf_op jit(solution)/shard_map/all_to_all | solution.py:159
